TPU v7x, 32 devices: a whole 2x2x4 slice. The times are simulated.
32 devices in a mesh: dp: 4 (over y, x), concept: 8 (over z, core).
Axes of the slice: x: 2, y: 2, z: 4, core: 2. Of those that a mesh axis runs over, the one named last changes fastest.
Arguments:
- embeddings: bfloat16 [32768, 1024], P(('dp', 'concept')), may hold values from -720 to 720
- row_weight: bfloat16 [32768], P(('dp', 'concept')), may hold values from 0.25 to 4
- group_label: int32 [32768, 1], P(('dp', 'concept')), may hold values from 0 to 7; in each aligned block of 1024 rows (0 to 1023, 1024 to 2047, ...) at most 256 rows name the same one
- concept_label: int32 [32768], P(('dp', 'concept')), may hold values from 0 to 1023
- level1_weight: bfloat16 [1024, 8], replicated, may hold values from -0.1875 to 0.1875
- level2_weight: bfloat16 [8, 1024, 1024], P('concept'), may hold values from -0.1875 to 0.1875
Outputs:
- row_loss: float32 [32768], P(('dp', 'concept'))
- embed_grad: bfloat16 [32768, 1024], P(('dp', 'concept'))
- level1_grad: float32 [1024, 8], replicated
- level2_grad: bfloat16 [8, 1024, 1024], P('concept', 'dp')
Inputs may be any that keep to these rules, and one draw needn't show every extreme that they name: `group_label`: among the rows of one device, no group is named more than 256 times, a bound that some block reaches.
All inputs are finite; a program needn't handle non-finite values.
Results may differ from a plain program's by a relative error of at most 0.0051.
Values may be sent and summed in bfloat16 or wider, within the bound.
No kernel may reach another device: no remote copies, remote signals or barrier semaphores. Data moves between devices by JAX's collectives and lax.ppermute only.
A program may use at most 128 MiB of HBM per device.

v0:
```python
import jax
import jax.numpy as jnp
from jax import lax
from jax.sharding import PartitionSpec as P


def first_level(embeddings, weights, groups, level1_weight):
    groups_n = level1_weight.shape[1]
    z1 = jnp.dot(embeddings, level1_weight, preferred_element_type=jnp.float32)
    top1 = jnp.max(z1, axis=1, keepdims=True)
    exps1 = jnp.exp(z1 - top1)
    total1 = jnp.sum(exps1, axis=1, keepdims=True)
    probs1 = exps1 / total1
    onehot1 = (groups[:, None] == jnp.arange(groups_n, dtype=jnp.int32)[None, :]).astype(
        jnp.float32
    )
    loss1 = top1[:, 0] + jnp.log(total1[:, 0]) - jnp.sum(z1 * onehot1, axis=1)
    dz1 = (weights[:, None] * (probs1 - onehot1)).astype(jnp.bfloat16)
    partial_grad = lax.dot_general(
        embeddings, dz1, (((0,), (0,)), ((), ())), preferred_element_type=jnp.float32
    )
    dx1 = jnp.dot(dz1, level1_weight.T, preferred_element_type=jnp.float32)
    level1_grad = lax.psum(partial_grad, ("dp", "concept"))
    return (loss1, dx1, level1_grad)


def on_device(embeddings, row_weight, group_label, concept_label, level1_weight, level2_weight):
    rows_n, width = embeddings.shape
    groups_n = level1_weight.shape[1]
    concepts = level2_weight.shape[2]
    capacity = 2 * rows_n // groups_n
    groups = group_label[:, 0]
    weights = row_weight.astype(jnp.float32)
    member = (groups[:, None] == jnp.arange(groups_n, dtype=jnp.int32)[None, :]).astype(
        jnp.bfloat16
    )
    positions = jnp.arange(rows_n, dtype=jnp.int32)
    earlier = (positions[None, :] < positions[:, None]).astype(jnp.bfloat16)
    before = jnp.dot(earlier, member, preferred_element_type=jnp.float32)
    rank = jnp.sum(before * member.astype(jnp.float32), axis=1).astype(jnp.int32)
    slot = groups * capacity + rank
    source = jnp.full((groups_n * capacity,), rows_n, jnp.int32).at[slot].set(positions)
    filled = source < rows_n
    safe = jnp.minimum(source, rows_n - 1)
    send_rows = jnp.where(filled[:, None], embeddings[safe], jnp.zeros((), jnp.bfloat16)).reshape(
        groups_n, capacity, width
    )
    send_weight = jnp.where(filled, row_weight[safe], jnp.zeros((), jnp.bfloat16)).reshape(
        groups_n, capacity
    )
    send_label = jnp.where(filled, concept_label[safe], 0).reshape(groups_n, capacity)
    loss1, dx1, level1_grad = first_level(embeddings, weights, groups, level1_weight)
    recv_rows, recv_weight, recv_label = (
        lax.all_to_all(send_rows, "concept", split_axis=0, concat_axis=1, tiled=True),
        lax.all_to_all(send_weight, "concept", split_axis=0, concat_axis=1, tiled=True),
        lax.all_to_all(send_label, "concept", split_axis=0, concat_axis=1, tiled=True),
    )
    z2 = jnp.einsum("grd,gdc->grc", recv_rows, level2_weight, preferred_element_type=jnp.float32)
    top2 = jnp.max(z2, axis=2, keepdims=True)
    exps2 = jnp.exp(z2 - top2)
    total2 = jnp.sum(exps2, axis=2, keepdims=True)
    probs2 = exps2 / total2
    onehot2 = (
        recv_label[:, :, None] == jnp.arange(concepts, dtype=jnp.int32)[None, None, :]
    ).astype(jnp.float32)
    loss2 = (top2[:, :, 0] + jnp.log(total2[:, :, 0]) - jnp.sum(z2 * onehot2, axis=2)).astype(
        jnp.bfloat16
    )
    dz2 = (recv_weight.astype(jnp.float32)[:, :, None] * (probs2 - onehot2)).astype(jnp.bfloat16)
    dx2 = jnp.einsum("grc,gdc->grd", dz2, level2_weight, preferred_element_type=jnp.float32).astype(
        jnp.bfloat16
    )
    back_grad, back_loss = (
        lax.all_to_all(dx2, "concept", split_axis=1, concat_axis=0, tiled=True),
        lax.all_to_all(loss2, "concept", split_axis=1, concat_axis=0, tiled=True),
    )
    summed = lax.psum_scatter(
        jnp.einsum("grd,grc->dgc", recv_rows, dz2, preferred_element_type=jnp.float32),
        "dp",
        scatter_dimension=0,
        tiled=True,
    )
    level2_grad = jnp.transpose(summed, (1, 0, 2)).astype(jnp.bfloat16)
    dx2_rows = back_grad.reshape(groups_n * capacity, width)[slot]
    loss2_rows = back_loss.reshape(groups_n * capacity)[slot]
    embed_grad = (dx1 + dx2_rows.astype(jnp.float32)).astype(jnp.bfloat16)
    row_loss = loss1 + loss2_rows.astype(jnp.float32)
    return (row_loss, embed_grad, level1_grad, level2_grad)


def solution(mesh):
    return jax.shard_map(
        on_device,
        mesh=mesh,
        in_specs=(
            P(("dp", "concept"), None),
            P(("dp", "concept")),
            P(("dp", "concept"), None),
            P(("dp", "concept")),
            P(),
            P("concept", None, None),
        ),
        out_specs=(P(("dp", "concept")), P(("dp", "concept"), None), P(), P("concept", "dp", None)),
        check_vma=False,
    )
```

profile of v0, /device:TPU:0, one launch (start us, length us, event | category | flops | bytes accessed | tf_op | source)
XLA Modules:
  0.0 421.7 jit_solution(6824636984605057728)
XLA Ops:
  7.2 1.3 fusion.6
  9.2 4.3 %scatter_custom_fusion = s32[2048]{0:T(1024)S(1)} fusion(s32[1024]{0:T(1024)S(1)} %bitcast.59, s32[1024]{0:T(1024)S(1)} %iota.19, s32[]{:T(128)} %constant.2.clone.1), kind=kCustom, calls=%fused_computation.39 | custom fusion | bytes 8196 | tf_op jit(solution)/shard_map/scatter | solution.py:42
  13.6 11.5 %gather_fusion.3 = bf16[2048]{0:T(1024)(128)(2,1)S(1)} fusion(bf16[1024]{0:T(1024)(128)(2,1)} %param.7, s32[2048]{0:T(1024)S(1)} %fusion.10), kind=kCustom, calls=%fused_computation.3 | custom fusion | bytes 16384 | tf_op jit(solution)/shard_map/gather | solution.py:48
  26.9 6.4 %all-to-all-start.3 = ((bf16[8,2,128]{2,1,0:T(2,128)(2,1)}), bf16[8,2,128]{2,1,0:T(2,128)(2,1)S(1)}, u32[]{:S(2)}, u32[]{:S(2)}) async-start(bf16[8,2,128]{2,1,0:T(2,128)(2,1)} %reshape.239), calls=%async_computation.3 | async-start | bytes 8192 | tf_op jit(solution)/shard_map/all_to_all | solution.py:55
  33.2 12.8 %gather_fusion = bf16[2048,1024]{1,0:T(8,128)(2,1)} fusion(bf16[1024,1024]{1,0:T(8,128)(2,1)} %param.6, s32[2048]{0:T(1024)S(1)} %fusion.10), kind=kCustom, calls=%fused_computation | custom fusion | bytes 8396800 | tf_op jit(solution)/shard_map/gather | solution.py:45
  46.1 3.8 broadcast_select_fusion
  49.9 5.2 %all-to-all-start = ((bf16[8,256,1024]{2,1,0:T(8,128)(2,1)}), bf16[8,256,1024]{2,1,0:T(8,128)(2,1)}, u32[]{:S(2)}, u32[]{:S(2)}) async-start(bf16[8,256,1024]{2,1,0:T(8,128)(2,1)} %broadcast_select_fusion), calls=%async_computation | async-start | bytes 8388608 | tf_op jit(solution)/shard_map/all_to_all | solution.py:54
  55.1 8.6 %gather_fusion.1 = s32[2048]{0:T(1024)S(1)} fusion(s32[1024]{0:T(1024)S(1)} %copy-done.2, s32[2048]{0:T(1024)S(1)} %fusion.10), kind=kCustom, calls=%fused_computation.1 | custom fusion | bytes 24576 | tf_op jit(solution)/shard_map/gather | solution.py:51
  64.3 84.9 %all-to-all-done = bf16[8,256,1024]{2,1,0:T(8,128)(2,1)} async-done(((bf16[8,256,1024]{2,1,0:T(8,128)(2,1)}), bf16[8,256,1024]{2,1,0:T(8,128)(2,1)}, u32[]{:S(2)}, u32[]{:S(2)}) %all-to-all-start) | async-done | bytes 4194336 | tf_op jit(solution)/shard_map/all_to_all | solution.py:54
  149.2 3.3 all-to-all-start.1
  152.6 9.0 %fusion.13 = (f32[2048]{0:T(1024)S(1)}, f32[2048,1024]{0,1:T(8,128)}) fusion(bf16[2048,1024]{1,0:T(8,128)(2,1)} %bitcast.4, bf16[1,1024,1024]{2,1,0:T(8,128)(2,1)S(1)} %copy-done), kind=kOutput, calls=%fused_computation.43 | convolution fusion | flops 4297062400 | bytes 14688256 | tf_op jit(solution)/shard_map/grd,gdc->grc/dot_general | solution.py:58
  161.6 4.7 %fusion = (f32[2048]{0:T(1024)S(1)}, f32[2048]{0:T(1024)S(1)}) fusion(f32[2048,1024]{0,1:T(8,128)} %get-tuple-element.27, f32[2048]{0:T(1024)S(1)} %get-tuple-element.26, s32[2048]{0:T(1024)S(1)} %bitcast.51), kind=kLoop, calls=%fused_computation.10 | loop fusion | flops 10481664 | bytes 8421376 | tf_op jit(solution)/shard_map/reduce_sum | solution.py:61
  166.3 1.1 copy-done.4
  167.4 2.6 multiply_convert_fusion
  170.1 1.9 copy-done.5
  172.0 8.2 %convolution_bitcast_fusion = f32[1024,1,1024]{0,2,1:T(8,128)} fusion(bf16[2048,1024]{0,1:T(8,128)(2,1)S(1)} %multiply_convert_fusion, bf16[2048,1024]{1,0:T(8,128)(2,1)} %bitcast.4), kind=kOutput, calls=%fused_computation.17 | convolution fusion | flops 4294967296 | bytes 12582912 | tf_op jit(solution)/shard_map/grd,grc->dgc/dot_general | solution.py:78
  181.4 5.0 %all-to-all-start.2 = ((bf16[8,2,128]{2,1,0:T(2,128)(2,1)}), bf16[8,2,128]{2,1,0:T(2,128)(2,1)S(1)}, u32[]{:S(2)}, u32[]{:S(2)}) async-start(bf16[8,2,128]{2,1,0:T(2,128)(2,1)} %reshape.237), calls=%async_computation.2 | async-start | bytes 8192 | tf_op jit(solution)/shard_map/all_to_all | solution.py:75
  186.4 7.5 %convert_bitcast_fusion = bf16[1,2048,1024]{2,1,0:T(8,128)(2,1)S(1)} fusion(bf16[2048,1024]{0,1:T(8,128)(2,1)} %copy-done.5, bf16[1,1024,1024]{2,1,0:T(8,128)(2,1)S(1)} %copy-done), kind=kOutput, calls=%fused_computation.13 | convolution fusion | flops 4297064448 | bytes 10485760 | tf_op jit(solution)/shard_map/grc,gdc->grd/dot_general | solution.py:70
  193.9 28.7 %copy.24 = bf16[1,2048,1024]{2,0,1:T(2,128)(2,1)} copy(bf16[1,2048,1024]{2,1,0:T(8,128)(2,1)S(1)} %convert_bitcast_fusion) | data formatting | bytes 8388608 | tf_op jit(solution)/shard_map/convert_element_type | solution.py:70
  222.6 26.0 %reduce.10 = bf16[2048,1024]{1,0:T(8,128)(2,1)} reduce(bf16[2048,1,1024]{2,1,0:T(2,128)(2,1)} %bitcast.48, bf16[]{:T(256)} %broadcast.72), dimensions={1}, to_apply=%bitcast.44.reduce_sub_computation | reduce | bytes 8388610
  248.6 7.8 %reshape.241 = bf16[8,2,131072]{2,1,0:T(2,128)(2,1)} reshape(bf16[2048,1024]{1,0:T(8,128)(2,1)} %reduce.10) | data formatting | bytes 8388608
  256.4 5.3 %all-to-all-start.4 = ((bf16[8,2,131072]{2,1,0:T(2,128)(2,1)}), bf16[8,2,131072]{2,1,0:T(2,128)(2,1)}, u32[]{:S(2)}, u32[]{:S(2)}) async-start(bf16[8,2,131072]{2,1,0:T(2,128)(2,1)} %reshape.241), calls=%async_computation.4 | async-start | bytes 8388608 | tf_op jit(solution)/shard_map/all_to_all | solution.py:74
  261.8 2.3 fusion.14
  264.1 2.0 convolution_bitcast_fusion.1
  266.1 110.7 %psum.7 = f32[1024,8]{0,1:T(8,128)} all-reduce(f32[1024,8]{0,1:T(8,128)S(1)} %convolution_bitcast_fusion.1), channel_id=1, replica_groups=mesh['dp'=4,'concept'=8] {'dp','concept'}, use_global_device_ids=true, to_apply=%region_8.9 | all-reduce | flops 8192 | bytes 65536 | tf_op jit(solution)/shard_map/psum | solution.py:23
  376.8 6.8 %gather_fusion.2 = bf16[1024]{0:T(1024)(128)(2,1)S(1)} fusion(bf16[2048]{0:T(1024)(128)(2,1)S(1)} %bitcast.46, s32[1024]{0:T(1024)S(1)} %broadcast_clamp_fusion), kind=kCustom, calls=%fused_computation.2 | custom fusion | bytes 8192 | tf_op jit(solution)/shard_map/gather | solution.py:85
  384.2 8.8 %reshape.242 = bf16[2048,1,1024]{2,1,0:T(2,128)(2,1)} reshape(bf16[8,2,131072]{2,1,0:T(2,128)(2,1)} %all-to-all-done.4) | data formatting | bytes 8388608
  393.0 7.0 %copy.23 = bf16[1,2048,1024]{2,1,0:T(8,128)(2,1)} copy(bf16[1,2048,1024]{2,0,1:T(2,128)(2,1)} %bitcast.49) | data formatting | bytes 8388608
  400.0 8.9 %gather_fusion.4 = bf16[1024,1024]{1,0:T(8,128)(2,1)} fusion(bf16[2048,1024]{1,0:T(8,128)(2,1)} %bitcast.47, s32[1024]{0:T(1024)S(1)} %broadcast_clamp_fusion), kind=kCustom, calls=%fused_computation.4 | custom fusion | bytes 4198400 | tf_op jit(solution)/shard_map/gather | solution.py:84
  408.9 3.7 add_convert_fusion
  412.6 1.3 convert_bitcast_fusion.1
  413.8 1.0 copy.18
  (45 shorter events, 5.3 us)
Async XLA Ops:
  7.2 145.4 %copy-start = (bf16[1,1024,1024]{2,1,0:T(8,128)(2,1)S(1)}, bf16[1,1024,1024]{2,1,0:T(8,128)(2,1)}, u32[]{:S(2)}) copy-start(bf16[1,1024,1024]{2,1,0:T(8,128)(2,1)} %param.11) | copy-start | bytes 6291460
  26.9 23.0 %all-to-all-start.3 = ((bf16[8,2,128]{2,1,0:T(2,128)(2,1)}), bf16[8,2,128]{2,1,0:T(2,128)(2,1)S(1)}, u32[]{:S(2)}, u32[]{:S(2)}) async-start(bf16[8,2,128]{2,1,0:T(2,128)(2,1)} %reshape.239), calls=%async_computation.3 | async-start | bytes 8192 | tf_op jit(solution)/shard_map/all_to_all | solution.py:55
  49.9 5.2 %copy-start.2 = (s32[1024]{0:T(1024)S(1)}, s32[1024]{0:T(1024)}, u32[]{:S(2)}) copy-start(s32[1024]{0:T(1024)} %param.9) | copy-start | bytes 12292
  49.9 99.3 %all-to-all-start = ((bf16[8,256,1024]{2,1,0:T(8,128)(2,1)}), bf16[8,256,1024]{2,1,0:T(8,128)(2,1)}, u32[]{:S(2)}, u32[]{:S(2)}) async-start(bf16[8,256,1024]{2,1,0:T(8,128)(2,1)} %broadcast_select_fusion), calls=%async_computation | async-start | bytes 8388608 | tf_op jit(solution)/shard_map/all_to_all | solution.py:54
  149.2 12.4 %all-to-all-start.1 = ((s32[8,1,256]{2,1,0:T(1,128)}), s32[8,1,256]{2,1,0:T(1,128)S(1)}, u32[]{:S(2)}, u32[]{:S(2)}) async-start(s32[8,1,256]{2,1,0:T(1,128)} %bitcast.6), calls=%async_computation.1 | async-start | bytes 16384 | tf_op jit(solution)/shard_map/all_to_all | solution.py:56
  152.5 260.0 %reduce-scatter.2.cloned.1.call-start = ((), (), s32[]{:S(2)}) async-start(), calls=%async_computation.6 | async-start | bytes 5242880 | tf_op jit(solution)/shard_map/reduce_scatter | solution.py:77
  161.6 5.8 %copy-start.4 = (f32[2048,1024]{0,1:T(8,128)S(1)}, f32[2048,1024]{0,1:T(8,128)}, u32[]{:S(2)}) copy-start(f32[2048,1024]{0,1:T(8,128)} %get-tuple-element.27) | copy-start | bytes 25165828
  170.0 1.9 copy-start.5
  181.4 75.0 %all-to-all-start.2 = ((bf16[8,2,128]{2,1,0:T(2,128)(2,1)}), bf16[8,2,128]{2,1,0:T(2,128)(2,1)S(1)}, u32[]{:S(2)}, u32[]{:S(2)}) async-start(bf16[8,2,128]{2,1,0:T(2,128)(2,1)} %reshape.237), calls=%async_computation.2 | async-start | bytes 8192 | tf_op jit(solution)/shard_map/all_to_all | solution.py:75
  256.4 5.3 %copy-start.3 = (bf16[1024]{0:T(1024)(128)(2,1)S(1)}, bf16[1024]{0:T(1024)(128)(2,1)}, u32[]{:S(2)}) copy-start(bf16[1024]{0:T(1024)(128)(2,1)} %param.7) | copy-start | bytes 6148
  256.4 5.4 %copy-start.6 = (bf16[1024,8]{0,1:T(8,128)(2,1)S(1)}, bf16[1024,8]{0,1:T(8,128)(2,1)}, u32[]{:S(2)}) copy-start(bf16[1024,8]{0,1:T(8,128)(2,1)} %param.10) | copy-start | bytes 49156
  256.4 7.6 %copy-start.7 = (s32[1024,1]{0,1:T(1,128)S(1)}, s32[1024,1]{0,1:T(1,128)}, u32[]{:S(2)}) copy-start(s32[1024,1]{0,1:T(1,128)} %param.8) | copy-start | bytes 12292
  256.4 127.8 %all-to-all-start.4 = ((bf16[8,2,131072]{2,1,0:T(2,128)(2,1)}), bf16[8,2,131072]{2,1,0:T(2,128)(2,1)}, u32[]{:S(2)}, u32[]{:S(2)}) async-start(bf16[8,2,131072]{2,1,0:T(2,128)(2,1)} %reshape.241), calls=%async_computation.4 | async-start | bytes 8388608 | tf_op jit(solution)/shard_map/all_to_all | solution.py:74
  400.0 14.8 %copy-start.1 = (bf16[1,1024,1024]{2,1,0:T(8,128)(2,1)S(1)}, bf16[1,1024,1024]{2,1,0:T(8,128)(2,1)}, u32[]{:S(2)}) copy-start(bf16[1,1024,1024]{2,1,0:T(8,128)(2,1)} %param.11) | copy-start | bytes 6291460
Sparse Core Ops, SparseCore 0:
  180.3 53.9 reduce-scatter.1
where the time goes:
time: 423 us; the launch traced here: 422 us
  local copies, waits for them, and re-layouts  111 us (26%)
  blocking collectives  111 us (26%)
  waiting for transfers between devices  84.9 us (20%)
  other arithmetic  41.7 us (10%)
  matrix products  33.9 us (8%)
  starting transfers between devices  25.3 us (6%)
  between operations  14.2 us (3%)
    psum x1, blocking collectives, first_level(): level1_grad = lax.psum(partial_grad, ('dp', 'concept'))  111 us
    all_to_all x1, waiting for transfers between devices, on_device(): lax.all_to_all(send_rows, 'concept', split_axis=0, concat_axis=1, tiled=T...  84.9 us
    unnamed x26, local copies, waits for them, and re-layouts  29.4 us
    convert_element_type x1, local copies, waits for them, and re-layouts, on_device(): jnp.einsum('grc,gdc->grd', dz2, level2_weight, preferred_element_type=jnp...  28.7 us
    unnamed x2, other arithmetic  26.6 us
    gather x1, local copies, waits for them, and re-layouts, on_device(): embeddings[safe]  12.8 us
    gather x1, local copies, waits for them, and re-layouts, on_device(): row_weight[safe]  11.5 us
    dot_general x1, matrix products, on_device(): jnp.einsum('grd,gdc->grc', recv_rows, level2_weight, preferred_element_ty...  9.01 us
  transfers between devices with their start and end apart: 6, of which 1 were waited for; matrix products, arithmetic and copies ran while one was open for 35% of the time, Pallas kernels for 0%

commit v1 on v0

--- a/solution.py
+++ b/solution.py
@@ -20,7 +20,7 @@
         embeddings, dz1, (((0,), (0,)), ((), ())), preferred_element_type=jnp.float32
     )
     dx1 = jnp.dot(dz1, level1_weight.T, preferred_element_type=jnp.float32)
-    level1_grad = lax.psum(partial_grad, ("dp", "concept"))
+    level1_grad = jnp.sum(lax.all_gather(partial_grad, axis_name=("dp", "concept")), axis=0)
     return (loss1, dx1, level1_grad)
 
 

time: 423 us -> 401 us (0.948)
  blocking collectives: 111 us -> 0 us
  waiting for transfers between devices: 84.9 us -> 170 us
    psum x1 -> x0, blocking collectives: 111 us -> none  [first_level(): level1_grad = lax.psum(partial_grad, ('dp', 'concept'))]
    all_to_all x1, waiting for transfers between devices: 0.01 us -> 84.7 us  [on_device(): lax.all_to_all(dx2, 'concept', split_axis=1, concat_axis=0, tiled=True)]
    unnamed x26 -> x24, local copies, waits for them, and re-layouts: 29.4 us -> 28.3 us
  transfers between devices with their start and end apart: 6 -> 7, of which waited for: 1 -> 2; matrix products, arithmetic and copies ran while one was open for 35% -> 41% of each run, Pallas kernels for 0% -> 0%
where the time goes in v1:
time: 401 us; the launch traced here: 400 us
  waiting for transfers between devices  170 us (42%)
  local copies, waits for them, and re-layouts  110 us (27%)
  other arithmetic  45.7 us (11%)
  matrix products  34.1 us (9%)
  starting transfers between devices  25.1 us (6%)
  between operations  15.7 us (4%)
    all_to_all x1, waiting for transfers between devices, on_device(): lax.all_to_all(send_rows, 'concept', split_axis=0, concat_axis=1, tiled=T...  84.8 us
    all_to_all x1, waiting for transfers between devices, on_device(): lax.all_to_all(dx2, 'concept', split_axis=1, concat_axis=0, tiled=True)  84.7 us
    convert_element_type x1, local copies, waits for them, and re-layouts, on_device(): jnp.einsum('grc,gdc->grd', dz2, level2_weight, preferred_element_type=jnp...  28.7 us
    unnamed x24, local copies, waits for them, and re-layouts  28.3 us
    unnamed x2, other arithmetic  26.6 us
    gather x1, local copies, waits for them, and re-layouts, on_device(): embeddings[safe]  12.8 us
    gather x1, local copies, waits for them, and re-layouts, on_device(): row_weight[safe]  11.5 us
    dot_general x1, matrix products, on_device(): jnp.einsum('grd,gdc->grc', recv_rows, level2_weight, preferred_element_ty...  9.01 us
  transfers between devices with their start and end apart: 7, of which 2 were waited for; matrix products, arithmetic and copies ran while one was open for 41% of the time, Pallas kernels for 0%

profile of v1, /device:TPU:0, one launch (start us, length us, event | category | flops | bytes accessed | tf_op | source)
XLA Modules:
  0.0 400.1 jit_solution(4026492664921054478)
XLA Ops:
  8.0 1.3 fusion.6
  10.1 4.3 %scatter_custom_fusion = s32[2048]{0:T(1024)S(1)} fusion(s32[1024]{0:T(1024)S(1)} %bitcast.61, s32[1024]{0:T(1024)S(1)} %iota.19, s32[]{:T(128)} %constant.2.clone.1), kind=kCustom, calls=%fused_computation.39 | custom fusion | bytes 8196 | tf_op jit(solution)/shard_map/scatter | solution.py:42
  14.4 11.5 %gather_fusion.3 = bf16[2048]{0:T(1024)(128)(2,1)S(1)} fusion(bf16[1024]{0:T(1024)(128)(2,1)} %param.7, s32[2048]{0:T(1024)S(1)} %fusion.10), kind=kCustom, calls=%fused_computation.3 | custom fusion | bytes 16384 | tf_op jit(solution)/shard_map/gather | solution.py:48
  27.7 6.4 %all-to-all-start.3 = ((bf16[8,2,128]{2,1,0:T(2,128)(2,1)}), bf16[8,2,128]{2,1,0:T(2,128)(2,1)S(1)}, u32[]{:S(2)}, u32[]{:S(2)}) async-start(bf16[8,2,128]{2,1,0:T(2,128)(2,1)} %reshape.240), calls=%async_computation.3 | async-start | bytes 8192 | tf_op jit(solution)/shard_map/all_to_all | solution.py:55
  34.1 12.8 %gather_fusion = bf16[2048,1024]{1,0:T(8,128)(2,1)} fusion(bf16[1024,1024]{1,0:T(8,128)(2,1)} %param.6, s32[2048]{0:T(1024)S(1)} %fusion.10), kind=kCustom, calls=%fused_computation | custom fusion | bytes 8396800 | tf_op jit(solution)/shard_map/gather | solution.py:45
  46.9 3.8 broadcast_select_fusion
  50.7 5.2 %all-to-all-start = ((bf16[8,256,1024]{2,1,0:T(8,128)(2,1)}), bf16[8,256,1024]{2,1,0:T(8,128)(2,1)}, u32[]{:S(2)}, u32[]{:S(2)}) async-start(bf16[8,256,1024]{2,1,0:T(8,128)(2,1)} %broadcast_select_fusion), calls=%async_computation | async-start | bytes 8388608 | tf_op jit(solution)/shard_map/all_to_all | solution.py:54
  56.0 2.3 fusion.14
  58.3 2.6 convolution_bitcast_fusion.1
  61.0 8.6 %gather_fusion.1 = s32[2048]{0:T(1024)S(1)} fusion(s32[1024]{0:T(1024)S(1)} %copy-done.2, s32[2048]{0:T(1024)S(1)} %fusion.10), kind=kCustom, calls=%fused_computation.1 | custom fusion | bytes 24576 | tf_op jit(solution)/shard_map/gather | solution.py:51
  70.2 84.8 %all-to-all-done = bf16[8,256,1024]{2,1,0:T(8,128)(2,1)} async-done(((bf16[8,256,1024]{2,1,0:T(8,128)(2,1)}), bf16[8,256,1024]{2,1,0:T(8,128)(2,1)}, u32[]{:S(2)}, u32[]{:S(2)}) %all-to-all-start) | async-done | bytes 4194336 | tf_op jit(solution)/shard_map/all_to_all | solution.py:54
  155.0 3.3 all-to-all-start.1
  158.4 9.0 %fusion.13 = (f32[2048]{0:T(1024)S(1)}, f32[2048,1024]{0,1:T(8,128)}) fusion(bf16[2048,1024]{1,0:T(8,128)(2,1)} %bitcast.4, bf16[1,1024,1024]{2,1,0:T(8,128)(2,1)S(1)} %copy-done), kind=kOutput, calls=%fused_computation.43 | convolution fusion | flops 4297062400 | bytes 14688256 | tf_op jit(solution)/shard_map/grd,gdc->grc/dot_general | solution.py:58
  167.4 4.6 %fusion = (f32[2048]{0:T(1024)S(1)}, f32[2048]{0:T(1024)S(1)}) fusion(f32[2048,1024]{0,1:T(8,128)} %get-tuple-element.27, f32[2048]{0:T(1024)S(1)} %get-tuple-element.26, s32[2048]{0:T(1024)S(1)} %bitcast.53), kind=kLoop, calls=%fused_computation.10 | loop fusion | flops 10481664 | bytes 8421376 | tf_op jit(solution)/shard_map/reduce_sum | solution.py:61
  173.3 5.0 %all-to-all-start.2 = ((bf16[8,2,128]{2,1,0:T(2,128)(2,1)}), bf16[8,2,128]{2,1,0:T(2,128)(2,1)S(1)}, u32[]{:S(2)}, u32[]{:S(2)}) async-start(bf16[8,2,128]{2,1,0:T(2,128)(2,1)} %reshape.238), calls=%async_computation.2 | async-start | bytes 8192 | tf_op jit(solution)/shard_map/all_to_all | solution.py:75
  178.6 4.8 %multiply_convert_fusion = bf16[2048,1024]{0,1:T(8,128)(2,1)S(1)} fusion(f32[2048,1024]{0,1:T(8,128)} %get-tuple-element.27, f32[2048]{0:T(1024)S(1)} %get-tuple-element.20, f32[2048]{0:T(1024)S(1)} %bitcast.59, s32[2048]{0:T(1024)S(1)} %bitcast.54, f32[2048]{0:T(1024)S(1)} %get-tuple-element.26), kind=kLoop, calls=%fused_computation.6 | loop fusion | flops 14680064 | bytes 12615680 | tf_op jit(solution)/shard_map/convert_element_type | solution.py:69
  183.4 1.9 copy-done.4
  185.3 8.2 %convolution_bitcast_fusion = f32[1024,1,1024]{0,2,1:T(8,128)} fusion(bf16[2048,1024]{0,1:T(8,128)(2,1)S(1)} %multiply_convert_fusion, bf16[2048,1024]{1,0:T(8,128)(2,1)} %bitcast.4), kind=kOutput, calls=%fused_computation.17 | convolution fusion | flops 4294967296 | bytes 12582912 | tf_op jit(solution)/shard_map/grd,grc->dgc/dot_general | solution.py:78
  193.5 7.0 %convert_bitcast_fusion = bf16[1,2048,1024]{2,1,0:T(8,128)(2,1)S(1)} fusion(bf16[2048,1024]{0,1:T(8,128)(2,1)} %copy-done.4, bf16[1,1024,1024]{2,1,0:T(8,128)(2,1)S(1)} %copy-done), kind=kOutput, calls=%fused_computation.13 | convolution fusion | flops 4297064448 | bytes 10485760 | tf_op jit(solution)/shard_map/grc,gdc->grd/dot_general | solution.py:70
  200.5 28.7 %copy.24 = bf16[1,2048,1024]{2,0,1:T(2,128)(2,1)} copy(bf16[1,2048,1024]{2,1,0:T(8,128)(2,1)S(1)} %convert_bitcast_fusion) | data formatting | bytes 8388608 | tf_op jit(solution)/shard_map/convert_element_type | solution.py:70
  229.2 26.0 %reduce.10 = bf16[2048,1024]{1,0:T(8,128)(2,1)} reduce(bf16[2048,1,1024]{2,1,0:T(2,128)(2,1)} %bitcast.49, bf16[]{:T(256)} %broadcast.72), dimensions={1}, to_apply=%bitcast.45.reduce_sub_computation | reduce | bytes 8388610
  255.2 7.8 %reshape.242 = bf16[8,2,131072]{2,1,0:T(2,128)(2,1)} reshape(bf16[2048,1024]{1,0:T(8,128)(2,1)} %reduce.10) | data formatting | bytes 8388608
  263.0 4.9 %all-to-all-start.4 = ((bf16[8,2,131072]{2,1,0:T(2,128)(2,1)}), bf16[8,2,131072]{2,1,0:T(2,128)(2,1)}, u32[]{:S(2)}, u32[]{:S(2)}) async-start(bf16[8,2,131072]{2,1,0:T(2,128)(2,1)} %reshape.242), calls=%async_computation.4 | async-start | bytes 8388608 | tf_op jit(solution)/shard_map/all_to_all | solution.py:74
  267.9 1.9 reduce_sum.59
  269.9 6.8 %gather_fusion.2 = bf16[1024]{0:T(1024)(128)(2,1)S(1)} fusion(bf16[2048]{0:T(1024)(128)(2,1)S(1)} %bitcast.47, s32[1024]{0:T(1024)S(1)} %broadcast_clamp_fusion), kind=kCustom, calls=%fused_computation.2 | custom fusion | bytes 8192 | tf_op jit(solution)/shard_map/gather | solution.py:85
  277.3 84.7 %all-to-all-done.4 = bf16[8,2,131072]{2,1,0:T(2,128)(2,1)} async-done(((bf16[8,2,131072]{2,1,0:T(2,128)(2,1)}), bf16[8,2,131072]{2,1,0:T(2,128)(2,1)}, u32[]{:S(2)}, u32[]{:S(2)}) %all-to-all-start.4) | async-done | bytes 4194336 | tf_op jit(solution)/shard_map/all_to_all | solution.py:74
  362.0 8.8 %reshape.243 = bf16[2048,1,1024]{2,1,0:T(2,128)(2,1)} reshape(bf16[8,2,131072]{2,1,0:T(2,128)(2,1)} %all-to-all-done.4) | data formatting | bytes 8388608
  370.7 7.0 %copy.23 = bf16[1,2048,1024]{2,1,0:T(8,128)(2,1)} copy(bf16[1,2048,1024]{2,0,1:T(2,128)(2,1)} %bitcast.50) | data formatting | bytes 8388608
  377.8 8.9 %gather_fusion.4 = bf16[1024,1024]{1,0:T(8,128)(2,1)} fusion(bf16[2048,1024]{1,0:T(8,128)(2,1)} %bitcast.48, s32[1024]{0:T(1024)S(1)} %broadcast_clamp_fusion), kind=kCustom, calls=%fused_computation.4 | custom fusion | bytes 4198400 | tf_op jit(solution)/shard_map/gather | solution.py:84
  386.6 3.7 add_convert_fusion
  390.3 1.3 convert_bitcast_fusion.1
  391.6 1.0 copy.18
  (46 shorter events, 5.5 us)
Async XLA Ops:
  8.0 150.4 %copy-start = (bf16[1,1024,1024]{2,1,0:T(8,128)(2,1)S(1)}, bf16[1,1024,1024]{2,1,0:T(8,128)(2,1)}, u32[]{:S(2)}) copy-start(bf16[1,1024,1024]{2,1,0:T(8,128)(2,1)} %param.11) | copy-start | bytes 6291460
  27.7 23.0 %all-to-all-start.3 = ((bf16[8,2,128]{2,1,0:T(2,128)(2,1)}), bf16[8,2,128]{2,1,0:T(2,128)(2,1)S(1)}, u32[]{:S(2)}, u32[]{:S(2)}) async-start(bf16[8,2,128]{2,1,0:T(2,128)(2,1)} %reshape.240), calls=%async_computation.3 | async-start | bytes 8192 | tf_op jit(solution)/shard_map/all_to_all | solution.py:55
  50.7 5.3 %copy-start.3 = (bf16[1024]{0:T(1024)(128)(2,1)S(1)}, bf16[1024]{0:T(1024)(128)(2,1)}, u32[]{:S(2)}) copy-start(bf16[1024]{0:T(1024)(128)(2,1)} %param.7) | copy-start | bytes 6148
  50.7 5.3 %copy-start.5 = (bf16[1024,8]{0,1:T(8,128)(2,1)S(1)}, bf16[1024,8]{0,1:T(8,128)(2,1)}, u32[]{:S(2)}) copy-start(bf16[1024,8]{0,1:T(8,128)(2,1)} %param.10) | copy-start | bytes 49156
  50.7 7.6 %copy-start.6 = (s32[1024,1]{0,1:T(1,128)S(1)}, s32[1024,1]{0,1:T(1,128)}, u32[]{:S(2)}) copy-start(s32[1024,1]{0,1:T(1,128)} %param.8) | copy-start | bytes 12292
  50.7 104.3 %all-to-all-start = ((bf16[8,256,1024]{2,1,0:T(8,128)(2,1)}), bf16[8,256,1024]{2,1,0:T(8,128)(2,1)}, u32[]{:S(2)}, u32[]{:S(2)}) async-start(bf16[8,256,1024]{2,1,0:T(8,128)(2,1)} %broadcast_select_fusion), calls=%async_computation | async-start | bytes 8388608 | tf_op jit(solution)/shard_map/all_to_all | solution.py:54
  55.9 5.0 %copy-start.2 = (s32[1024]{0:T(1024)S(1)}, s32[1024]{0:T(1024)}, u32[]{:S(2)}) copy-start(s32[1024]{0:T(1024)} %param.9) | copy-start | bytes 12292
  56.0 212.0 %all-gather.3.cloned.1.call-start = ((), (), s32[]{:S(2)}) async-start(), calls=%async_computation.7 | async-start | bytes 1081344 | tf_op jit(solution)/shard_map/all_gather | solution.py:23
  155.0 12.4 %all-to-all-start.1 = ((s32[8,1,256]{2,1,0:T(1,128)}), s32[8,1,256]{2,1,0:T(1,128)S(1)}, u32[]{:S(2)}, u32[]{:S(2)}) async-start(s32[8,1,256]{2,1,0:T(1,128)} %bitcast.6), calls=%async_computation.1 | async-start | bytes 16384 | tf_op jit(solution)/shard_map/all_to_all | solution.py:56
  173.3 89.7 %all-to-all-start.2 = ((bf16[8,2,128]{2,1,0:T(2,128)(2,1)}), bf16[8,2,128]{2,1,0:T(2,128)(2,1)S(1)}, u32[]{:S(2)}, u32[]{:S(2)}) async-start(bf16[8,2,128]{2,1,0:T(2,128)(2,1)} %reshape.238), calls=%async_computation.2 | async-start | bytes 8192 | tf_op jit(solution)/shard_map/all_to_all | solution.py:75
  178.3 212.0 %reduce-scatter.2.cloned.1.call-start = ((), (), s32[]{:S(2)}) async-start(), calls=%async_computation.6 | async-start | bytes 5242880 | tf_op jit(solution)/shard_map/reduce_scatter | solution.py:77
  183.4 1.9 copy-start.4
  263.0 98.9 %all-to-all-start.4 = ((bf16[8,2,131072]{2,1,0:T(2,128)(2,1)}), bf16[8,2,131072]{2,1,0:T(2,128)(2,1)}, u32[]{:S(2)}, u32[]{:S(2)}) async-start(bf16[8,2,131072]{2,1,0:T(2,128)(2,1)} %reshape.242), calls=%async_computation.4 | async-start | bytes 8388608 | tf_op jit(solution)/shard_map/all_to_all | solution.py:74
  377.8 14.8 %copy-start.1 = (bf16[1,1024,1024]{2,1,0:T(8,128)(2,1)S(1)}, bf16[1,1024,1024]{2,1,0:T(8,128)(2,1)}, u32[]{:S(2)}) copy-start(bf16[1,1024,1024]{2,1,0:T(8,128)(2,1)} %param.11) | copy-start | bytes 6291460
Sparse Core Ops, SparseCore 0:
  61.1 75.1 all-gather.2
Sparse Core Ops, SparseCore 1:
  193.6 53.7 reduce-scatter.1
